TPU v7x, 32 devices: a whole 2x2x4 slice. The times are simulated.
32 devices in a mesh: ens: 2 (over y), wide: 4 (over z), lev: 2 (over x), fld: 2 (over core).
Axes of the slice: x: 2, y: 2, z: 4, core: 2. Of those that a mesh axis runs over, the one named last changes fastest.
Arguments:
- fourier_input_rows: bfloat16 [4, 1280, 4, 4, 256], P('ens', 'wide', None, 'fld', 'lev'), parts along dimension 0, may hold values from -6 to 6
- legendre: bfloat16 [4, 1280, 1280], P('wide', ('lev', 'fld')), may hold values from -0.15625 to 0.15625
- slot_wave: int32 [4], P('wide'), may hold values from 0 to 1279, as said below
- to_modes: bfloat16 [128, 128], replicated, may hold values from -0.5 to 0.5
- from_modes: bfloat16 [128, 128], replicated, may hold values from -0.5 to 0.5
- mode_rate: float32 [128], replicated, may hold values from 0.05 to 5
Outputs:
- fourier_out: bfloat16 [4, 1280, 4, 4, 256], P('ens', 'wide', None, 'fld', 'lev'), parts along dimension 0
- spectral: bfloat16 [8, 1280, 4, 256], P(('ens', 'wide'), None, 'fld', 'lev'), parts along dimension 0
There are 2 independent parts, one for each index of `ens`. A program takes and returns all parts, laid end to end along the dimension named above; an argument that names none is the same for every part. Nothing has to cross between parts.
Inputs may be any that keep to these rules, and one draw needn't show every extreme that they name: `slot_wave`: the wavenumbers of the slots are distinct; one slot holds 0 and one holds 1279.
All inputs are finite; a program needn't handle non-finite values.
Results may differ from a plain program's by a relative error of at most 0.0065.
Values may be sent and summed in bfloat16 or wider, within the bound.
A program may use at most 64 MiB of HBM per device.

v0:
```python
import math
import jax
import jax.numpy as jnp
from jax import lax
from jax.sharding import PartitionSpec as P


def latitude_weights(count):
    position = jnp.arange(count, dtype=jnp.float32)
    return jnp.sin(math.pi * (position + 0.5) / (2 * count))


def project(level_grid, degree_real, weight_rows, rate_rows, degree_total):
    projected = jnp.einsum(
        "kl,snflr->snfkr", weight_rows, level_grid, preferred_element_type=jnp.float32
    )
    factor = 1.0 + degree_real[:, None] * (degree_real[:, None] + 1.0) * rate_rows[None, :] / (
        degree_total * degree_total
    )
    return (projected / factor[None, :, None, :, None]).astype(jnp.bfloat16)


def shards(fourier_input_rows, legendre, slot_wave, to_modes, from_modes, mode_rate):
    wave_rows = lax.all_to_all(fourier_input_rows, "wide", split_axis=2, concat_axis=1, tiled=True)
    half_count = wave_rows.shape[1]
    slot_count = wave_rows.shape[2]
    field_count = wave_rows.shape[3]
    column_count = wave_rows.shape[4]
    degree_count = legendre.shape[1] * lax.axis_size(("lev", "fld"))
    weights = latitude_weights(half_count)[:, None, None, None]
    north_half = wave_rows[0].astype(jnp.float32)
    south_half = wave_rows[1].astype(jnp.float32)
    symmetric = (weights * (north_half + south_half)).astype(jnp.bfloat16)
    antisym = (weights * (north_half - south_half)).astype(jnp.bfloat16)
    paired = jnp.concatenate((symmetric, antisym), axis=3)

    def direct_rows(section, first_row):
        row_count = section.shape[1]
        degree = first_row + jnp.arange(row_count, dtype=jnp.int32)
        relative = degree[None, :] - slot_wave[:, None]
        product = jnp.einsum("snj,jsfc->snfc", section, paired, preferred_element_type=jnp.float32)
        is_even = (relative % 2 == 0)[:, :, None, None]
        is_live = (relative >= 0)[:, :, None, None]
        picked = jnp.where(is_even, product[..., :column_count], product[..., column_count:])
        return jnp.where(is_live, picked, jnp.zeros_like(picked))

    full_table = lax.all_gather(legendre, ("lev", "fld"), axis=1, tiled=True)
    block_rows = 128
    block_count = degree_count // block_rows

    def direct_step(block_index, buffer):
        first_row = block_index * block_rows
        section = lax.dynamic_slice_in_dim(full_table, first_row, block_rows, 1)
        result = direct_rows(section, first_row).astype(jnp.bfloat16)
        return lax.dynamic_update_slice_in_dim(buffer, result, first_row, 1)

    initial_raw = jnp.zeros((slot_count, degree_count, field_count, column_count), jnp.bfloat16)
    raw_spectral = lax.fori_loop(0, block_count, direct_step, initial_raw)
    own_levels = column_count // 2
    first_level = lax.axis_index("lev") * own_levels
    degree_real = jnp.arange(degree_count, dtype=jnp.float32)
    all_levels = lax.all_gather(raw_spectral, "lev", axis=3, tiled=True)
    level_count = all_levels.shape[3] // 2
    level_grid = all_levels.reshape(slot_count, degree_count, field_count, level_count, 2)
    weight_rows = lax.dynamic_slice_in_dim(to_modes, first_level, own_levels, 0)
    rate_rows = lax.dynamic_slice_in_dim(mode_rate, first_level, own_levels, 0)
    own_modes = project(level_grid, degree_real, weight_rows, rate_rows, degree_count).reshape(
        slot_count, degree_count, field_count, column_count
    )
    mode_values = lax.all_gather(own_modes, "lev", axis=3, tiled=True).reshape(
        slot_count, degree_count, field_count, level_count, 2
    )
    back_rows = lax.dynamic_slice_in_dim(from_modes, first_level, own_levels, 0)
    spectral = jnp.einsum(
        "lk,snfkr->snflr", back_rows, mode_values, preferred_element_type=jnp.float32
    )
    spectral = spectral.astype(jnp.bfloat16).reshape(
        slot_count, degree_count, field_count, column_count
    )

    def inverse_rows(running, section, first_row):
        row_count = section.shape[1]
        degree = first_row + jnp.arange(row_count, dtype=jnp.int32)
        relative = degree[None, :] - slot_wave[:, None]
        spec_rows = lax.dynamic_slice_in_dim(spectral, first_row, row_count, 1)
        even_mask = ((relative >= 0) & (relative % 2 == 0))[:, :, None, None]
        odd_mask = ((relative >= 0) & (relative % 2 == 1))[:, :, None, None]
        empty_rows = jnp.zeros_like(spec_rows)
        parity_split = jnp.concatenate(
            (
                jnp.where(even_mask, spec_rows, empty_rows),
                jnp.where(odd_mask, spec_rows, empty_rows),
            ),
            axis=3,
        )
        return running + jnp.einsum(
            "snj,snfc->jsfc", section, parity_split, preferred_element_type=jnp.float32
        )

    initial_sum = jnp.zeros((half_count, slot_count, field_count, 2 * column_count), jnp.float32)

    def inverse_step(block_index, running):
        first_row = block_index * block_rows
        section = lax.dynamic_slice_in_dim(full_table, first_row, block_rows, 1)
        return inverse_rows(running, section, first_row)

    running = lax.fori_loop(0, block_count, inverse_step, initial_sum)
    even_sum = running[..., :column_count]
    odd_sum = running[..., column_count:]
    fourier_wave = jnp.stack((even_sum + odd_sum, even_sum - odd_sum), axis=0).astype(jnp.bfloat16)
    fourier_out = lax.all_to_all(fourier_wave, "wide", split_axis=1, concat_axis=2, tiled=True)
    return (fourier_out, spectral)


def solution(mesh):
    in_specs = (
        P("ens", "wide", None, "fld", "lev"),
        P("wide", ("lev", "fld"), None),
        P("wide"),
        P(),
        P(),
        P(),
    )
    out_specs = (P("ens", "wide", None, "fld", "lev"), P(("ens", "wide"), None, "fld", "lev"))
    return jax.shard_map(shards, mesh=mesh, in_specs=in_specs, out_specs=out_specs, check_vma=False)
```

profile of v0, /device:TPU:0, one launch (start us, length us, event | category | flops | bytes accessed | tf_op | source)
XLA Modules:
  0.0 206.5 jit_solution(15960541568794821746)
XLA Ops:
  7.9 3.3 %copy.24 = bf16[2,320,4,2,128]{4,3,1,0,2:T(2,128)(2,1)} copy(bf16[2,320,4,2,128]{4,3,2,1,0:T(2,128)(2,1)} %param.10) | data formatting | bytes 2621440 | tf_op args[0]
  11.2 6.3 %all-to-all-start = ((bf16[2,320,4,2,128]{4,3,1,0,2:T(2,128)(2,1)}), bf16[2,320,4,2,128]{4,3,1,0,2:T(2,128)(2,1)S(1)}, u32[]{:S(2)}, u32[]{:S(2)}) async-start(bf16[2,320,4,2,128]{4,3,1,0,2:T(2,128)(2,1)} %copy.24), calls=%async_computation | async-start | bytes 2621440 | tf_op jit(solution)/shard_map/all_to_all | solution.py:24
  17.6 31.3 %all-to-all-done = bf16[2,320,4,2,128]{4,3,1,0,2:T(2,128)(2,1)S(1)} async-done(((bf16[2,320,4,2,128]{4,3,1,0,2:T(2,128)(2,1)}), bf16[2,320,4,2,128]{4,3,1,0,2:T(2,128)(2,1)S(1)}, u32[]{:S(2)}, u32[]{:S(2)}) %all-to-all-start) | async-done | bytes 1310752 | tf_op jit(solution)/shard_map/all_to_all | solution.py:24
  50.3 21.4 %while.31 = (s32[]{:T(128)}, bf16[1,1280,2,128]{3,1,2,0:T(8,128)(2,1)S(1)}, s32[1]{0:T(128)}, bf16[1,1280,1280]{2,1,0:T(8,128)(2,1)}, bf16[1280,1,2,256]{3,0,2,1...) while((s32[]{:T(128)}, bf16[1,1280,2,128]{3,1,2,0:T(8,128)(2,1)S(1)}, s32[1]{0:T(128)}, ...), condition=%wide.region_1.2_spmd, body=%wide.region_0.1_spmd.sunk | while | flops 167839616 | bytes 1967515 | solution.py:58
  56.8 1.3 fusion.47
  58.9 1.3 fusion.47
  61.1 1.3 fusion.47
  63.2 1.3 fusion.47
  65.3 1.3 fusion.47
  72.9 23.2 %all-gather.6.cloned.1.call-done = bf16[1,1280,2,256]{3,1,2,0:T(8,128)(2,1)} async-done(((bf16[1,1280,2,128]{3,1,2,0:T(8,128)(2,1)}), bf16[1,1280,2,256]{3,1,2,0:T(8,128)(2,1)}) %all-gather.6.cloned.1.call-update) | async-done | bytes 1310736 | tf_op jit(solution)/shard_map/all_gather | solution.py:62
  96.1 3.6 %copy.27 = bf16[1,1280,2,256]{1,2,3,0:T(2,128)(2,1)S(1)} copy(bf16[1,1280,2,256]{3,1,2,0:T(8,128)(2,1)} %all-gather.6.cloned.1.call-done) | data formatting | bytes 2621440 | tf_op jit(solution)/shard_map/all_gather | solution.py:62
  100.1 1.5 copy.29
  101.6 24.4 %all-gather.8.cloned.1.call-done = bf16[1,1280,2,256]{1,2,0,3:T(2,128)(2,1)} async-done(((bf16[1,1280,2,128]{1,2,0,3:T(2,128)(2,1)}), bf16[1,1280,2,256]{1,2,0,3:T(2,128)(2,1)}) %all-gather.8.cloned.1.call-update) | async-done | bytes 1310736 | tf_op jit(solution)/shard_map/all_gather | solution.py:70
  126.0 1.6 fusion.22
  128.4 25.0 %while.32 = (s32[]{:T(128)}, f32[1280,1,2,256]{0,3,2,1:T(8,128)S(1)}, s32[1]{0:T(128)}, bf16[1,1280,2,128]{1,2,3,0:T(2,128)(2,1)S(1)}, bf16[1,1280,1280]{2,1,0:T...) while((s32[]{:T(128)}, f32[1280,1,2,256]{0,3,2,1:T(8,128)S(1)}, s32[1]{0:T(128)}, ...), condition=%wide.region_3.4_spmd.clone, body=%wide.region_2.3_spmd.clone.sunk | while | flops 169412864 | bytes 6029989 | solution.py:107
  129.1 1.7 fusion.51
  131.6 1.7 fusion.51
  134.1 1.7 fusion.51
  136.6 1.7 fusion.51
  139.1 1.7 fusion.51
  141.6 1.7 fusion.51
  144.1 1.7 fusion.51
  146.6 1.7 fusion.51
  149.1 1.7 fusion.51
  151.6 1.7 fusion.51
  153.4 3.1 %copy.34 = f32[1280,1,2,256]{3,2,0,1:T(2,128)} copy(f32[1280,1,2,256]{0,3,2,1:T(8,128)S(1)} %get-tuple-element.269) | data formatting | bytes 5242880 | tf_op jit(solution)/shard_map/while | solution.py:107
  156.5 2.2 %fusion.30 = (bf16[1,1280,1,2,128]{4,3,0,2,1:T(2,128)(2,1)S(1)}, bf16[1,1280,1,2,128]{4,3,0,2,1:T(2,128)(2,1)S(1)}) fusion(f32[1280,1,2,256]{3,2,0,1:T(2,128)} %copy.34), kind=kLoop, calls=%fused_computation.54 | loop fusion | flops 1310720 | bytes 3932160 | tf_op jit(solution)/shard_map/stack | solution.py:110
  158.7 2.7 %pad_maximum_fusion.1 = bf16[2,1280,1,2,128]{4,3,0,2,1:T(2,128)(2,1)} fusion(bf16[1,1280,1,2,128]{4,3,0,2,1:T(2,128)(2,1)S(1)} %get-tuple-element.334, bf16[1,1280,1,2,128]{4,3,0,2,1:T(2,128)(2,1)S(1)} %get-tuple-element.333), kind=kLoop, calls=%fused_computation.45 | loop fusion | flops 655360 | bytes 2621440 | tf_op jit(solution)/shard_map/stack | solution.py:110
  161.5 4.6 %all-to-all-start.1 = ((bf16[2,1280,1,2,128]{4,3,0,2,1:T(2,128)(2,1)}), bf16[2,1280,1,2,128]{4,3,0,2,1:T(2,128)(2,1)S(1)}, u32[]{:S(2)}, u32[]{:S(2)}) async-start(bf16[2,1280,1,2,128]{4,3,0,2,1:T(2,128)(2,1)} %pad_maximum_fusion.1), calls=%async_computation.1 | async-start | bytes 2621440 | tf_op jit(solution)/shard_map/all_to_all | solution.py:111
  166.1 2.1 %copy.39 = bf16[1,1280,2,128]{3,2,1,0:T(2,128)(2,1)} copy(bf16[1,1280,2,128]{1,2,3,0:T(2,128)(2,1)S(1)} %get-tuple-element.472) | data formatting | bytes 1310720
  168.2 29.2 %all-to-all-done.1 = bf16[2,1280,1,2,128]{4,3,0,2,1:T(2,128)(2,1)S(1)} async-done(((bf16[2,1280,1,2,128]{4,3,0,2,1:T(2,128)(2,1)}), bf16[2,1280,1,2,128]{4,3,0,2,1:T(2,128)(2,1)S(1)}, u32[]{:S(2)}, u32[]{:S(2)}) %all-to-all-start.1) | async-done | bytes 1310752 | tf_op jit(solution)/shard_map/all_to_all | solution.py:111
  197.6 2.4 %copy.38 = bf16[2,320,4,2,128]{4,3,2,1,0:T(2,128)(2,1)} copy(bf16[2,320,4,2,128]{4,1,2,3,0:T(8,128)(2,1)S(1)} %bitcast.88) | data formatting | bytes 2621440
  (82 shorter events, 26.3 us)
Async XLA Ops:
  7.2 92.5 %copy-start = (bf16[128,128]{1,0:T(8,128)(2,1)S(1)}, bf16[128,128]{1,0:T(8,128)(2,1)}, u32[]{:S(2)}) copy-start(bf16[128,128]{1,0:T(8,128)(2,1)} %param.13) | copy-start | bytes 98308
  7.2 43.1 %all-gather.4.cloned.1.call-start = ((), (), s32[]{:S(2)}) async-start(), calls=%async_computation.2 | async-start | bytes 4096000 | tf_op jit(solution)/shard_map/all_gather | solution.py:47
  11.2 37.7 %all-to-all-start = ((bf16[2,320,4,2,128]{4,3,1,0,2:T(2,128)(2,1)}), bf16[2,320,4,2,128]{4,3,1,0,2:T(2,128)(2,1)S(1)}, u32[]{:S(2)}, u32[]{:S(2)}) async-start(bf16[2,320,4,2,128]{4,3,1,0,2:T(2,128)(2,1)} %copy.24), calls=%async_computation | async-start | bytes 2621440 | tf_op jit(solution)/shard_map/all_to_all | solution.py:24
  17.5 78.6 %all-gather.6.cloned.1.call-start = ((), (), s32[]{:S(2)}) async-start(), calls=%async_computation.3 | async-start | bytes 1966080 | tf_op jit(solution)/shard_map/all_gather | solution.py:62
  50.3 22.3 %copy-start.3 = (f32[128]{0:T(128)S(1)}, f32[128]{0:T(128)}, u32[]{:S(2)}) copy-start(f32[128]{0:T(128)} %param.15) | copy-start | bytes 1540
  71.7 0.8 copy-start.1
  72.6 53.4 %all-gather.8.cloned.1.call-start = ((), (), s32[]{:S(2)}) async-start(), calls=%async_computation.4 | async-start | bytes 1966080 | tf_op jit(solution)/shard_map/all_gather | solution.py:70
  100.1 26.0 %copy-start.2 = (bf16[128,128]{1,0:T(8,128)(2,1)S(1)}, bf16[128,128]{1,0:T(8,128)(2,1)}, u32[]{:S(2)}) copy-start(bf16[128,128]{1,0:T(8,128)(2,1)} %param.14) | copy-start | bytes 98308
  161.5 35.9 %all-to-all-start.1 = ((bf16[2,1280,1,2,128]{4,3,0,2,1:T(2,128)(2,1)}), bf16[2,1280,1,2,128]{4,3,0,2,1:T(2,128)(2,1)S(1)}, u32[]{:S(2)}, u32[]{:S(2)}) async-start(bf16[2,1280,1,2,128]{4,3,0,2,1:T(2,128)(2,1)} %pad_maximum_fusion.1), calls=%async_computation.1 | async-start | bytes 2621440 | tf_op jit(solution)/shard_map/all_to_all | solution.py:111
Sparse Core Ops, SparseCore 0:
  9.6 31.9 all-gather.3
  72.7 23.3 all-gather.5
  101.7 24.2 all-gather.7
where the time goes:
time: 208 us; the launch traced here: 207 us
  waiting for transfers between devices  109 us (52%)
  matrix products  32.3 us (16%)
  other arithmetic  21.1 us (10%)
  local copies, waits for them, and re-layouts  18.4 us (9%)
  between operations  13.9 us (7%)
  starting transfers between devices  11 us (5%)
    all_to_all x1, waiting for transfers between devices, shards(): lax.all_to_all(fourier_input_rows, 'wide', split_axis=2, concat_axis=1, t...  31.3 us
    all_to_all x1, waiting for transfers between devices, shards(): lax.all_to_all(fourier_wave, 'wide', split_axis=1, concat_axis=2, tiled=T...  29.2 us
    all_gather x1, waiting for transfers between devices, shards(): lax.all_gather(own_modes, 'lev', axis=3, tiled=True)  24.4 us
    all_gather x1, waiting for transfers between devices, shards(): all_levels = lax.all_gather(raw_spectral, 'lev', axis=3, tiled=True)  23.2 us
    dot_general x10, matrix products, inverse_rows(): jnp.einsum('snj,snfc->jsfc', section, parity_split, preferred_element_typ...  17.2 us
    dot_general x10, matrix products, direct_rows(): jnp.einsum('snj,jsfc->snfc', section, paired, preferred_element_type=jnp....  13.2 us
    unnamed x11, local copies, waits for them, and re-layouts  8.65 us
    and x10, other arithmetic, inverse_rows(): odd_mask = ((relative >= 0) & (relative % 2 == 1))[:, :, None, None]  6.62 us
  transfers between devices with their start and end apart: 5, of which 4 were waited for; matrix products, arithmetic and copies ran while one was open for 3% of the time, Pallas kernels for 0%

commit v1 on v0

--- a/solution.py
+++ b/solution.py
@@ -3,6 +3,17 @@
 import jax.numpy as jnp
 from jax import lax
 from jax.sharding import PartitionSpec as P
+
+
+def cut_along(array, dim, size):
+    before, after = (array.shape[:dim], array.shape[dim + 1 :])
+    return jnp.moveaxis(array.reshape(*before, size, -1, *after), dim, 0)
+
+
+def in_order(pieces, dim):
+    dims = list(pieces.shape[1:])
+    dims[dim] *= pieces.shape[0]
+    return jnp.moveaxis(pieces, 0, dim).reshape(dims)
 
 
 def latitude_weights(count):
@@ -108,7 +119,14 @@
     even_sum = running[..., :column_count]
     odd_sum = running[..., column_count:]
     fourier_wave = jnp.stack((even_sum + odd_sum, even_sum - odd_sum), axis=0).astype(jnp.bfloat16)
-    fourier_out = lax.all_to_all(fourier_wave, "wide", split_axis=1, concat_axis=2, tiled=True)
+    size, index = (lax.axis_size("wide"), lax.axis_index("wide"))
+    parts = cut_along(fourier_wave, 1, size)
+    outs = [parts[index]]
+    for step in range(1, size):
+        sent = parts[(index + step) % size]
+        outs.append(lax.ppermute(sent, "wide", [(i, (i + step) % size) for i in range(size)]))
+    parts = jnp.stack(outs)[(index - jnp.arange(size)) % size]
+    fourier_out = in_order(parts, 2)
     return (fourier_out, spectral)
 
 

time: 208 us -> 201 us (0.966)
  the two profiles are of different devices: /device:TPU:0 before, /device:TPU:9 now
where the time goes in v1:
time: 201 us; the launch traced here: 199 us
  waiting for transfers between devices  105 us (52%)
  matrix products  32.3 us (16%)
  other arithmetic  19.3 us (10%)
  local copies, waits for them, and re-layouts  18.8 us (9%)
  between operations  14 us (7%)
  starting transfers between devices  8.48 us (4%)
    all_to_all x1, waiting for transfers between devices, shards(): lax.all_to_all(fourier_input_rows, 'wide', split_axis=2, concat_axis=1, t...  27.4 us
    all_gather x1, waiting for transfers between devices, shards(): all_levels = lax.all_gather(raw_spectral, 'lev', axis=3, tiled=True)  27.1 us
    ppermute x3, waiting for transfers between devices, shards(): lax.ppermute(sent, 'wide', [(i, (i + step) % size) for i in range(size)])  25.9 us
    all_gather x1, waiting for transfers between devices, shards(): lax.all_gather(own_modes, 'lev', axis=3, tiled=True)  24.3 us
    dot_general x10, matrix products, inverse_rows(): jnp.einsum('snj,snfc->jsfc', section, parity_split, preferred_element_typ...  17.2 us
    dot_general x10, matrix products, direct_rows(): jnp.einsum('snj,jsfc->snfc', section, paired, preferred_element_type=jnp....  13.2 us
    unnamed x13, local copies, waits for them, and re-layouts  9.4 us
    and x10, other arithmetic, inverse_rows(): odd_mask = ((relative >= 0) & (relative % 2 == 1))[:, :, None, None]  6.62 us
  transfers between devices with their start and end apart: 7, of which 6 were waited for; matrix products, arithmetic and copies ran while one was open for 4% of the time, Pallas kernels for 0%

profile of v1, /device:TPU:9, one launch (start us, length us, event | category | flops | bytes accessed | tf_op | source)
XLA Modules:
  0.0 199.3 jit_solution(1589768890174600567)
XLA Ops:
  7.9 3.3 %copy.27 = bf16[2,320,4,2,128]{4,3,1,0,2:T(2,128)(2,1)} copy(bf16[2,320,4,2,128]{4,3,2,1,0:T(2,128)(2,1)} %param.10) | data formatting | bytes 2621440 | tf_op args[0]
  11.2 4.8 %all-to-all-start = ((bf16[2,320,4,2,128]{4,3,1,0,2:T(2,128)(2,1)}), bf16[2,320,4,2,128]{4,3,1,0,2:T(2,128)(2,1)S(1)}, u32[]{:S(2)}, u32[]{:S(2)}) async-start(bf16[2,320,4,2,128]{4,3,1,0,2:T(2,128)(2,1)} %copy.27), calls=%async_computation | async-start | bytes 2621440 | tf_op jit(solution)/shard_map/all_to_all | solution.py:35
  16.0 27.4 %all-to-all-done = bf16[2,320,4,2,128]{4,3,1,0,2:T(2,128)(2,1)S(1)} async-done(((bf16[2,320,4,2,128]{4,3,1,0,2:T(2,128)(2,1)}), bf16[2,320,4,2,128]{4,3,1,0,2:T(2,128)(2,1)S(1)}, u32[]{:S(2)}, u32[]{:S(2)}) %all-to-all-start) | async-done | bytes 1310752 | tf_op jit(solution)/shard_map/all_to_all | solution.py:35
  44.9 21.4 %while.31 = (s32[]{:T(128)}, bf16[1,1280,2,128]{3,1,2,0:T(8,128)(2,1)S(1)}, s32[1]{0:T(128)}, bf16[1,1280,1280]{2,1,0:T(8,128)(2,1)}, bf16[1280,1,2,256]{3,0,2,1...) while((s32[]{:T(128)}, bf16[1,1280,2,128]{3,1,2,0:T(8,128)(2,1)S(1)}, s32[1]{0:T(128)}, ...), condition=%wide.region_1.2_spmd, body=%wide.region_0.1_spmd.sunk | while | flops 167839616 | bytes 1967515 | solution.py:69
  47.0 1.3 fusion.55
  49.2 1.3 fusion.55
  51.3 1.3 fusion.55
  53.5 1.3 fusion.55
  55.6 1.3 fusion.55
  67.4 27.1 %all-gather.6.cloned.1.call-done = bf16[1,1280,2,256]{3,1,2,0:T(8,128)(2,1)} async-done(((bf16[1,1280,2,128]{3,1,2,0:T(8,128)(2,1)}), bf16[1,1280,2,256]{3,1,2,0:T(8,128)(2,1)}) %all-gather.6.cloned.1.call-update) | async-done | bytes 1310736 | tf_op jit(solution)/shard_map/all_gather | solution.py:73
  94.6 3.6 %copy.30 = bf16[1,1280,2,256]{1,2,3,0:T(2,128)(2,1)S(1)} copy(bf16[1,1280,2,256]{3,1,2,0:T(8,128)(2,1)} %all-gather.6.cloned.1.call-done) | data formatting | bytes 2621440 | tf_op jit(solution)/shard_map/all_gather | solution.py:73
  98.5 1.5 copy.32
  100.1 24.3 %all-gather.8.cloned.1.call-done = bf16[1,1280,2,256]{1,2,0,3:T(2,128)(2,1)} async-done(((bf16[1,1280,2,128]{1,2,0,3:T(2,128)(2,1)}), bf16[1,1280,2,256]{1,2,0,3:T(2,128)(2,1)}) %all-gather.8.cloned.1.call-update) | async-done | bytes 1310736 | tf_op jit(solution)/shard_map/all_gather | solution.py:81
  124.5 1.6 fusion.22
  126.8 25.0 %while.32 = (s32[]{:T(128)}, f32[1280,1,2,256]{0,3,2,1:T(8,128)S(1)}, s32[1]{0:T(128)}, bf16[1,1280,2,128]{1,2,3,0:T(2,128)(2,1)S(1)}, bf16[1,1280,1280]{2,1,0:T...) while((s32[]{:T(128)}, f32[1280,1,2,256]{0,3,2,1:T(8,128)S(1)}, s32[1]{0:T(128)}, ...), condition=%wide.region_3.4_spmd.clone, body=%wide.region_2.3_spmd.clone.sunk | while | flops 169412864 | bytes 6029989 | solution.py:118
  127.6 1.7 fusion.59
  130.1 1.7 fusion.59
  132.6 1.7 fusion.59
  135.1 1.7 fusion.59
  137.6 1.7 fusion.59
  140.1 1.7 fusion.59
  142.6 1.7 fusion.59
  145.1 1.7 fusion.59
  147.6 1.7 fusion.59
  150.1 1.7 fusion.59
  151.8 2.1 %copy.37 = f32[1280,1,2,256]{3,0,2,1:T(8,128)} copy(f32[1280,1,2,256]{0,3,2,1:T(8,128)S(1)} %get-tuple-element.269) | data formatting | bytes 5242880 | tf_op jit(solution)/shard_map/while | solution.py:118
  154.0 1.9 subtract_convert_fusion
  159.7 2.1 %copy.44 = bf16[1,1280,2,128]{3,2,1,0:T(2,128)(2,1)} copy(bf16[1,1280,2,128]{1,2,3,0:T(2,128)(2,1)S(1)} %get-tuple-element.475) | data formatting | bytes 1310720
  161.8 2.8 %collective-permute-done = bf16[2,320,1,2,128]{4,1,3,0,2:T(8,128)(2,1)S(1)} collective-permute-done((bf16[2,320,1,2,128]{4,1,3,0,2:T(8,128)(2,1)S(1)}, bf16[2,320,1,2,128]{4,1,3,0,2:T(8,128)(2,1)S(1)}, u32[]{:S(2)}, u32[]{:S(2)}) %collective-permute-start) | collective-permute-done | bytes 327712 | tf_op jit(solution)/shard_map/ppermute | solution.py:127
  164.7 20.2 %collective-permute-done.1 = bf16[2,320,1,2,128]{4,1,3,0,2:T(8,128)(2,1)S(1)} collective-permute-done((bf16[2,320,1,2,128]{4,1,3,0,2:T(8,128)(2,1)S(1)}, bf16[2,320,1,2,128]{4,1,3,0,2:T(8,128)(2,1)S(1)}, u32[]{:S(2)}, u32[]{:S(2)}) %collective-permute-start.1) | collective-permute-done | bytes 327712 | tf_op jit(solution)/shard_map/ppermute | solution.py:127
  184.8 2.9 %collective-permute-done.2 = bf16[2,320,1,2,128]{4,1,3,0,2:T(8,128)(2,1)S(1)} collective-permute-done((bf16[2,320,1,2,128]{4,1,3,0,2:T(8,128)(2,1)S(1)}, bf16[2,320,1,2,128]{4,1,3,0,2:T(8,128)(2,1)S(1)}, u32[]{:S(2)}, u32[]{:S(2)}) %collective-permute-start.2) | collective-permute-done | bytes 327712 | tf_op jit(solution)/shard_map/ppermute | solution.py:127
  190.4 2.4 %copy.43 = bf16[2,320,4,2,128]{4,3,2,1,0:T(2,128)(2,1)} copy(bf16[2,320,4,2,128]{4,1,3,0,2:T(8,128)(2,1)S(1)} %bitcast.107) | data formatting | bytes 2621440
  (91 shorter events, 32.6 us)
Async XLA Ops:
  7.2 91.0 %copy-start = (bf16[128,128]{1,0:T(8,128)(2,1)S(1)}, bf16[128,128]{1,0:T(8,128)(2,1)}, u32[]{:S(2)}) copy-start(bf16[128,128]{1,0:T(8,128)(2,1)} %param.13) | copy-start | bytes 98308
  7.2 37.6 %all-gather.4.cloned.1.call-start = ((), (), s32[]{:S(2)}) async-start(), calls=%async_computation.1 | async-start | bytes 4096000 | tf_op jit(solution)/shard_map/all_gather | solution.py:58
  11.2 32.2 %all-to-all-start = ((bf16[2,320,4,2,128]{4,3,1,0,2:T(2,128)(2,1)}), bf16[2,320,4,2,128]{4,3,1,0,2:T(2,128)(2,1)S(1)}, u32[]{:S(2)}, u32[]{:S(2)}) async-start(bf16[2,320,4,2,128]{4,3,1,0,2:T(2,128)(2,1)} %copy.27), calls=%async_computation | async-start | bytes 2621440 | tf_op jit(solution)/shard_map/all_to_all | solution.py:35
  15.9 78.6 %all-gather.6.cloned.1.call-start = ((), (), s32[]{:S(2)}) async-start(), calls=%async_computation.2 | async-start | bytes 1966080 | tf_op jit(solution)/shard_map/all_gather | solution.py:73
  44.9 22.3 %copy-start.4 = (f32[128]{0:T(128)S(1)}, f32[128]{0:T(128)}, u32[]{:S(2)}) copy-start(f32[128]{0:T(128)} %param.15) | copy-start | bytes 1540
  66.3 0.8 copy-start.1
  67.1 57.3 %all-gather.8.cloned.1.call-start = ((), (), s32[]{:S(2)}) async-start(), calls=%async_computation.3 | async-start | bytes 1966080 | tf_op jit(solution)/shard_map/all_gather | solution.py:81
  98.5 26.0 %copy-start.3 = (bf16[128,128]{1,0:T(8,128)(2,1)S(1)}, bf16[128,128]{1,0:T(8,128)(2,1)}, u32[]{:S(2)}) copy-start(bf16[128,128]{1,0:T(8,128)(2,1)} %param.14) | copy-start | bytes 98308
  156.0 8.6 %collective-permute-start = (bf16[2,320,1,2,128]{4,1,3,0,2:T(8,128)(2,1)S(1)}, bf16[2,320,1,2,128]{4,1,3,0,2:T(8,128)(2,1)S(1)}, u32[]{:S(2)}, u32[]{:S(2)}) collective-permute-start(bf16[2,320,1,2,128]{4,1,3,0,2:T(8,128)(2,1)S(1)} %get-tuple-element.336), channel_id=1, source_target_pairs={{0,4},{4,8},{8,12},{12,0},{1,5},{5,9},{9,13},{13,1},{2,6},{6,10},{... | collective-permute-start | bytes 983048 | tf_op jit(solution)/shard_map/ppermute | solution.py:127
  157.3 27.5 %collective-permute-start.1 = (bf16[2,320,1,2,128]{4,1,3,0,2:T(8,128)(2,1)S(1)}, bf16[2,320,1,2,128]{4,1,3,0,2:T(8,128)(2,1)S(1)}, u32[]{:S(2)}, u32[]{:S(2)}) collective-permute-start(bf16[2,320,1,2,128]{4,1,3,0,2:T(8,128)(2,1)S(1)} %get-tuple-element.337), channel_id=1, source_target_pairs={{0,8},{4,12},{8,0},{12,4},{1,9},{5,13},{9,1},{13,5},{2,10},{6,14},... | collective-permute-start | bytes 983048 | tf_op jit(solution)/shard_map/ppermute | solution.py:127
  158.4 29.3 %collective-permute-start.2 = (bf16[2,320,1,2,128]{4,1,3,0,2:T(8,128)(2,1)S(1)}, bf16[2,320,1,2,128]{4,1,3,0,2:T(8,128)(2,1)S(1)}, u32[]{:S(2)}, u32[]{:S(2)}) collective-permute-start(bf16[2,320,1,2,128]{4,1,3,0,2:T(8,128)(2,1)S(1)} %get-tuple-element.338), channel_id=1, source_target_pairs={{0,12},{4,0},{8,4},{12,8},{1,13},{5,1},{9,5},{13,9},{2,14},{6,2},{... | collective-permute-start | bytes 983048 | tf_op jit(solution)/shard_map/ppermute | solution.py:127
  187.7 0.7 copy-start.2
Sparse Core Ops, SparseCore 0:
  9.6 30.8 all-gather.3
  67.3 27.2 all-gather.5
  100.2 24.2 all-gather.7
